TPU v7x, 32 devices: a whole 2x2x4 slice. The times are simulated.
32 devices in a mesh: section: 4 (over y, x), scen: 8 (over z, core).
Axes of the slice: x: 2, y: 2, z: 4, core: 2. Of those that a mesh axis runs over, the one named last changes fastest.
Arguments:
- right_side: float32 [4, 8, 512, 1024], P('section', 'scen'), may hold values from -6 to 6
- inverse_raw: bfloat16 [4, 8, 1024, 1024], P('section', 'scen'), may hold values from -0.1875 to 0.1875
- inverse_pattern: int32 [4, 8, 16, 16], P('section', 'scen'), may hold values 0 or 1
- coupling: bfloat16 [4, 8, 1024, 1024], P('section', 'scen'), may hold values from -0.1875 to 0.1875
- coupling_pattern: int32 [4, 8, 16, 16], P('section', 'scen'), may hold values 0 or 1
- pivots: float32 [4, 8, 1024], P('section', 'scen'), may hold values from 0.5 to 2
- offsets: int32 [4, 8], replicated, may hold values from 0 to 1, as said below
- above_solution: bfloat16 [8, 512, 1024], P('scen'), may hold values from -6 to 6
Outputs:
- solution: float32 [4, 8, 512, 1024], P('section', 'scen')
Inputs may be any that keep to these rules, and one draw needn't show every extreme that they name: Node c of level l has node c + offsets[l, c] of level l - 1 as its parent, and for l = 0 row c + offsets[0, c] of above_solution; offsets[l, 0] is 1 and offsets[l, 7] is 0 for every l.
All inputs are finite; a program needn't handle non-finite values. No bound on the sum of `inverse_pattern` or of `coupling_pattern` on one device may be relied on, other than what follows from the above.
Results may differ from a plain program's by a relative error of at most 0.0075.
Values may be sent and summed in bfloat16 or wider, within the bound.
A program may use at most 64 MiB of HBM per device.

v0:
```python
import functools

import jax
import jax.numpy as jnp
from jax import lax
from jax.experimental import pallas as pl
from jax.experimental.pallas import tpu as pltpu
from jax.sharding import PartitionSpec as P

ROWS = 32
LAG = 8
TILE = 256
MESH = pl.DeviceIdType.MESH


def dot_nn(a, b):
    return lax.dot_general(a, b, (((1,), (0,)), ((), ())), preferred_element_type=jnp.float32)


def kernel(
    levels,
    nodes,
    rows,
    given_ref,
    raw_ref,
    pattern_ref,
    coupling_ref,
    coupling_pattern_ref,
    pivot_ref,
    offsets_ref,
    above_ref,
    out_ref,
    factor,
    link,
    factor_t,
    link_t,
    kept,
    up_in,
    up_out,
    side_in,
    side_out,
    dside_in,
    dside_out,
    down_in,
    down_out,
    above_side,
    up_sems,
    side_sems,
    dside_sems,
    down_sems,
    above_sems,
):
    s = lax.axis_index("section")
    j = lax.axis_index("scen")
    total, features = given_ref.shape
    pieces = total // rows
    blocks = pattern_ref.shape[0]
    size = features // blocks
    has_up, has_down = s > 0, s < levels - 1
    has_left, has_right = j > 0, j < nodes - 1
    up_id = {"section": lax.rem(s + levels - 1, levels)}
    down_id = {"section": lax.rem(s + 1, levels)}
    right_id = {"scen": lax.rem(j + 1, nodes)}
    left_id = {"scen": lax.rem(j + nodes - 1, nodes)}

    barrier = pltpu.get_barrier_semaphore()
    count = jnp.int32(0)
    for has, where_to in ((has_up, up_id), (has_down, down_id), (has_left, left_id), (has_right, right_id)):

        @pl.when(has)
        def _(where_to=where_to):
            pl.semaphore_signal(barrier, inc=1, device_id=where_to, device_id_type=MESH)

        count = count + has.astype(jnp.int32)
    pl.semaphore_wait(barrier, count)

    def slot(ref, p):
        return ref.at[pl.ds(pl.multiple_of(p * rows, rows), rows), :]

    def copy(src, dst, sems, p, device):
        return pltpu.make_async_remote_copy(
            src_ref=slot(src, p),
            dst_ref=slot(dst, p),
            send_sem=sems.at[0, p],
            recv_sem=sems.at[1, p],
            device_id=device,
            device_id_type=MESH,
        )

    def up_copy(p):
        return copy(up_out, up_in, up_sems, p, up_id)

    def side_copy(p):
        return copy(side_out, side_in, side_sems, p, right_id)

    def dside_copy(p):
        return copy(dside_out, dside_in, dside_sems, p, left_id)

    def down_copy(p):
        return copy(down_out, down_in, down_sems, p, down_id)

    def above_copy():
        return pltpu.make_async_remote_copy(
            src_ref=above_ref,
            dst_ref=above_side,
            send_sem=above_sems.at[0],
            recv_sem=above_sems.at[1],
            device_id=left_id,
            device_id_type=MESH,
        )

    first = s == 0

    @pl.when(first & has_left)
    def _():
        above_copy().start()

    @pl.when(jnp.logical_not(has_down))
    def _():
        up_in[...] = jnp.zeros_like(up_in)

    @pl.when(jnp.logical_not(has_left))
    def _():
        side_in[...] = jnp.zeros_like(side_in)

    @pl.when(jnp.logical_not(has_right))
    def _():
        dside_in[...] = jnp.zeros_like(dside_in)
        above_side[...] = jnp.zeros_like(above_side)

    spread = (
        lax.broadcasted_iota(jnp.int32, (blocks, features), 1) // size
        == lax.broadcasted_iota(jnp.int32, (blocks, features), 0)
    ).astype(jnp.bfloat16)
    factor_mask = dot_nn(pattern_ref[...].astype(jnp.float32).astype(jnp.bfloat16), spread)
    link_mask = dot_nn(coupling_pattern_ref[...].astype(jnp.float32).astype(jnp.bfloat16), spread)
    col_ids = lax.broadcasted_iota(jnp.int32, (size, features), 1)
    for i in range(blocks):
        part = pl.ds(i * size, size)
        row_ids = lax.broadcasted_iota(jnp.int32, (size, features), 0) + i * size
        keep = (factor_mask[i : i + 1, :] > 0.5) & (row_ids > col_ids)
        unit = jnp.where(row_ids == col_ids, 1.0, 0.0)
        factor[part, :] = jnp.where(keep, raw_ref[part, :].astype(jnp.float32), unit).astype(jnp.bfloat16)
        link[part, :] = jnp.where(
            link_mask[i : i + 1, :] > 0.5, coupling_ref[part, :].astype(jnp.float32), 0.0
        ).astype(jnp.bfloat16)

    tile = min(TILE, features)
    for m in range(0, features, tile):
        for n in range(0, features, tile):
            if m >= n:
                factor_t[n : n + tile, m : m + tile] = factor[m : m + tile, n : n + tile].T
            link_t[n : n + tile, m : m + tile] = link[m : m + tile, n : n + tile].T

    own_offset = offsets_ref[s, j]
    left_offset = offsets_ref[s, jnp.maximum(j - 1, 0)]
    child_offset = offsets_ref[jnp.minimum(s + 1, levels - 1), j]

    def forward(p):
        @pl.when(has_down)
        def _():
            up_copy(p).wait_recv()

        here = pl.ds(pl.multiple_of(p * rows, rows), rows)
        reduced = (given_ref[here, :] - up_in[here, :].astype(jnp.float32)).astype(jnp.bfloat16)
        result = jnp.concatenate(
            [
                dot_nn(reduced[:, : n + tile], factor_t[: n + tile, n : n + tile])
                for n in range(0, features, tile)
            ],
            axis=1,
        )
        kept[here, :] = result * pivot_ref[...]

        @pl.when(has_up)
        def _():
            side_out[here, :] = dot_nn(result.astype(jnp.bfloat16), link_t[...]).astype(jnp.bfloat16)

            @pl.when(has_right)
            def _():
                side_copy(p).start()

    def combine(p):
        @pl.when(has_up)
        def _():
            @pl.when(has_left)
            def _():
                side_copy(p).wait_recv()

            here = pl.ds(pl.multiple_of(p * rows, rows), rows)
            own = jnp.where(own_offset == 0, side_out[here, :].astype(jnp.float32), 0.0)
            moved = jnp.where(left_offset == 1, side_in[here, :].astype(jnp.float32), 0.0)
            up_out[here, :] = (own + jnp.where(has_left, moved, 0.0)).astype(jnp.bfloat16)
            up_copy(p).start()

    def backward(p):
        @pl.when(has_up)
        def _():
            down_copy(p).wait_recv()

        here = pl.ds(pl.multiple_of(p * rows, rows), rows)
        reduced = (kept[here, :] - dot_nn(down_in[here, :], link[...])).astype(jnp.bfloat16)
        result = jnp.concatenate(
            [dot_nn(reduced[:, n:], factor[n:, n : n + tile]) for n in range(0, features, tile)], axis=1
        )
        out_ref[here, :] = result

        @pl.when(has_down)
        def _():
            dside_out[here, :] = result.astype(jnp.bfloat16)

            @pl.when(has_left)
            def _():
                dside_copy(p).start()

    def select(p):
        @pl.when(has_down)
        def _():
            @pl.when(has_right)
            def _():
                dside_copy(p).wait_recv()

            here = pl.ds(pl.multiple_of(p * rows, rows), rows)
            down_out[here, :] = jnp.where(
                child_offset == 1,
                dside_in[here, :].astype(jnp.float32),
                dside_out[here, :].astype(jnp.float32),
            ).astype(jnp.bfloat16)
            down_copy(p).start()

    @pl.when(first)
    def _():
        @pl.when(has_right)
        def _():
            above_copy().wait_recv()

        down_in[...] = jnp.where(
            own_offset == 1, above_side[...].astype(jnp.float32), above_ref[...].astype(jnp.float32)
        ).astype(jnp.bfloat16)

    lag = jnp.minimum(LAG * s, pieces)

    def turn(u, carry):
        @pl.when(u < pieces)
        def _():
            forward(u)

        @pl.when((u >= 1) & (u <= pieces))
        def _():
            combine(u - 1)

        v = u - lag

        @pl.when((v >= 0) & (v < pieces))
        def _():
            backward(v)

        @pl.when((v >= 1) & (v <= pieces))
        def _():
            select(v - 1)

        return carry

    lax.fori_loop(0, pieces + lag + 1, turn, 0)

    def finish(p, carry):
        @pl.when(has_up)
        def _():
            up_copy(p).wait_send()

            @pl.when(has_right)
            def _():
                side_copy(p).wait_send()

        @pl.when(has_down)
        def _():
            down_copy(p).wait_send()

            @pl.when(has_left)
            def _():
                dside_copy(p).wait_send()

        return carry

    lax.fori_loop(0, pieces, finish, 0)

    @pl.when(first & has_left)
    def _():
        above_copy().wait_send()


def local(
    right_side,
    inverse_raw,
    inverse_pattern,
    coupling,
    coupling_pattern,
    pivots,
    offsets,
    above_solution,
):
    levels = lax.axis_size("section")
    nodes = lax.axis_size("scen")
    total, features = right_side.shape[2:]
    rows = min(ROWS, total)
    pieces = total // rows
    vmem = pl.BlockSpec(memory_space=pltpu.VMEM)
    half = pltpu.VMEM((total, features), jnp.bfloat16)
    square = pltpu.VMEM((features, features), jnp.bfloat16)
    sems = pltpu.SemaphoreType.DMA((2, pieces))
    solved = pl.pallas_call(
        functools.partial(kernel, levels, nodes, rows),
        out_shape=pltpu.VMEM((total, features), jnp.float32),
        in_specs=[vmem] * 6 + [pl.BlockSpec(memory_space=pltpu.SMEM), vmem],
        out_specs=vmem,
        scratch_shapes=[square] * 4 + [pltpu.VMEM((total, features), jnp.float32)]
        + [half] * 9
        + [sems] * 4
        + [pltpu.SemaphoreType.DMA((2,))],
        compiler_params=pltpu.CompilerParams(
            collective_id=0, has_side_effects=True, vmem_limit_bytes=60 * 1024 * 1024
        ),
    )(
        right_side[0, 0],
        inverse_raw[0, 0],
        inverse_pattern[0, 0],
        coupling[0, 0],
        coupling_pattern[0, 0],
        pivots[0],
        offsets,
        above_solution[0],
    )
    return solved[None, None]


def solution(mesh):
    placed = (
        P("section", "scen", None, None),
        P("section", "scen", None, None),
        P("section", "scen", None, None),
        P("section", "scen", None, None),
        P("section", "scen", None, None),
        P("section", "scen", None),
        P(),
        P("scen", None, None),
    )
    return jax.shard_map(
        local,
        mesh=mesh,
        in_specs=placed,
        out_specs=P("section", "scen", None, None),
        check_vma=False,
    )
```

profile of v0, /device:TPU:7, one launch (start us, length us, event | category | flops | bytes accessed | tf_op | source)
XLA Modules:
  0.0 81.9 jit_solution(13927257645074690652)
XLA Ops:
  0.0 80.6 %shard_map.82 = f32[512,1024]{1,0:T(8,128)S(1)} custom-call(f32[512,1024]{1,0:T(8,128)} %bitcast.9, bf16[1024,1024]{1,0:T(8,128)(2,1)} %bitcast.10, s32[16,16]{1,0:T(8,128)} %bitcast.13, bf16[1024,1024]{1,0:T(8,128)(2,1)} %bitcast.11, s32[16,16]{1,0:T(8,128)} %bitcast.14, f32[1,1024]{1,0:T(1,128)} %bitcast.15, s32[4,8]{1,0:T(4,128)} %offsets_ref.1, ...), custom_call_target="tpu_custom_call" | custom-call | tf_op jit(solution)/shard_map/pallas_call | solution.py:311
  80.6 1.3 %copy.10 = f32[1,1,512,1024]{3,2,1,0:T(8,128)} copy(f32[1,1,512,1024]{3,2,1,0:T(8,128)S(1)} %bitcast.8) | data formatting | bytes 4194304
where the time goes:
time: 82 us; the launch traced here: 81.9 us
  Pallas kernels  80.6 us (98%)
  local copies, waits for them, and re-layouts  1.32 us (2%)
    pallas_call x1, Pallas kernels, local(): pl.pallas_call(functools.partial(kernel, levels, nodes, rows), out_shape=...  80.6 us

commit v1 on v0

v1 whole, which is shorter than its diff:
```python
import functools

import jax
import jax.numpy as jnp
from jax import lax
from jax.experimental import pallas as pl
from jax.experimental.pallas import tpu as pltpu
from jax.sharding import PartitionSpec as P

ROWS = 32
BATCH = 128
TILE = 256
LANE = 128
AHEAD = 2
LAG = 7
LAG_STEP = 7
MESH = pl.DeviceIdType.MESH


def dot_nn(a, b):
    return lax.dot_general(a, b, (((1,), (0,)), ((), ())), preferred_element_type=jnp.float32)


def dot_nt(a, b):
    return lax.dot_general(a, b, (((1,), (1,)), ((), ())), preferred_element_type=jnp.float32)


def kernel(
    levels,
    nodes,
    rows,
    given_hbm,
    raw_hbm,
    pattern_ref,
    coupling_hbm,
    coupling_pattern_ref,
    pivot_ref,
    offsets_ref,
    above_hbm,
    out_ref,
    given,
    factor,
    link,
    gain,
    gain_t,
    inner,
    scaled_t,
    kept,
    red,
    up_out,
    up_own,
    up_side,
    dn_out,
    dn_own,
    dn_side,
    load_sems,
    up_sems,
    up_side_sems,
    dn_sems,
    dn_side_sems,
    above_sems,
):
    s = lax.axis_index("section")
    j = lax.axis_index("scen")
    total, features = given.shape
    pieces = total // rows
    batch = min(BATCH, total)
    blocks = pattern_ref.shape[0]
    size = features // blocks
    tile = min(TILE, features)
    tiles = range(0, features, tile)
    top, bottom = s == 0, s == levels - 1
    middle = jnp.logical_not(top | bottom)
    has_up, has_down = s > 0, s < levels - 1
    has_left, has_right = j > 0, j < nodes - 1
    up_id = {"section": lax.rem(s + levels - 1, levels)}
    down_id = {"section": lax.rem(s + 1, levels)}
    right_id = {"scen": lax.rem(j + 1, nodes)}
    left_id = {"scen": lax.rem(j + nodes - 1, nodes)}

    loads = [
        pltpu.make_async_copy(raw_hbm, factor, load_sems.at[0]),
        pltpu.make_async_copy(given_hbm, given, load_sems.at[1]),
        pltpu.make_async_copy(coupling_hbm, link, load_sems.at[2]),
    ]
    for load in loads:
        load.start()
    load_above = pltpu.make_async_copy(above_hbm, dn_own, load_sems.at[3])

    @pl.when(top)
    def _():
        load_above.start()

    barrier = pltpu.get_barrier_semaphore()
    count = jnp.int32(0)
    for has, where_to in ((has_up, up_id), (has_down, down_id), (has_left, left_id), (has_right, right_id)):

        @pl.when(has)
        def _(where_to=where_to):
            pl.semaphore_signal(barrier, inc=1, device_id=where_to, device_id_type=MESH)

        count = count + has.astype(jnp.int32)

    def piece(p):
        return pl.ds(pl.multiple_of(p * rows, rows), rows)

    def copy(src, dst, sems, p, device):
        return pltpu.make_async_remote_copy(
            src_ref=src.at[piece(p), :],
            dst_ref=dst.at[piece(p), :],
            send_sem=sems.at[0, p],
            recv_sem=sems.at[1, p],
            device_id=device,
            device_id_type=MESH,
        )

    def up_copy(p):
        return copy(up_out, up_own, up_sems, p, up_id)

    def up_relay(p):
        return copy(up_own, up_side, up_side_sems, p, right_id)

    def dn_copy(p):
        return copy(dn_out, dn_own, dn_sems, p, down_id)

    def dn_relay(p):
        return copy(dn_own, dn_side, dn_side_sems, p, left_id)

    def above_copy():
        return pltpu.make_async_remote_copy(
            src_ref=dn_own,
            dst_ref=dn_side,
            send_sem=above_sems.at[0],
            recv_sem=above_sems.at[1],
            device_id=left_id,
            device_id_type=MESH,
        )

    @pl.when(jnp.logical_not(has_left))
    def _():
        up_side[...] = jnp.zeros_like(up_side)

    @pl.when(jnp.logical_not(has_right))
    def _():
        dn_side[...] = jnp.zeros_like(dn_side)

    spread = (
        lax.broadcasted_iota(jnp.int32, (blocks, features), 1) // size
        == lax.broadcasted_iota(jnp.int32, (blocks, features), 0)
    ).astype(jnp.bfloat16)
    factor_mask = dot_nn(pattern_ref[...].astype(jnp.float32).astype(jnp.bfloat16), spread)
    link_mask = dot_nn(coupling_pattern_ref[...].astype(jnp.float32).astype(jnp.bfloat16), spread)
    loads[0].wait()
    for i in range(blocks):
        part = pl.ds(i * size, size)
        low = i * size // LANE * LANE
        high = (i * size // tile + 1) * tile
        if low > 0:
            mask = jnp.broadcast_to(factor_mask[i : i + 1, :low], (size, low)).astype(jnp.bfloat16)
            factor[part, :low] = factor[part, :low] * mask
        row_ids = lax.broadcasted_iota(jnp.int32, (size, LANE), 0) + i * size
        col_ids = lax.broadcasted_iota(jnp.int32, (size, LANE), 1) + low
        keep = (factor_mask[i : i + 1, low : low + LANE] > 0.5) & (row_ids > col_ids)
        unit = jnp.where(row_ids == col_ids, 1.0, 0.0)
        diagonal = factor[part, low : low + LANE].astype(jnp.float32)
        factor[part, low : low + LANE] = jnp.where(keep, diagonal, unit).astype(jnp.bfloat16)
        if high > low + LANE:
            factor[part, low + LANE : high] = jnp.zeros((size, high - low - LANE), jnp.bfloat16)
    loads[2].wait()
    for i in range(blocks):
        part = pl.ds(i * size, size)
        mask = jnp.broadcast_to(link_mask[i : i + 1, :], (size, features)).astype(jnp.bfloat16)
        link[part, :] = link[part, :] * mask
    loads[1].wait()
    pl.semaphore_wait(barrier, count)

    @pl.when(top)
    def _():
        load_above.wait()

        @pl.when(has_left)
        def _():
            above_copy().start()

    def big(b):
        return pl.ds(pl.multiple_of(b * batch, batch), batch)

    @pl.when(bottom)
    def _():
        def first(b, carry):
            here = big(b)
            given_rows = given[here, :].astype(jnp.bfloat16)
            forward = jnp.concatenate(
                [dot_nt(given_rows[:, : n + tile], factor[n : n + tile, : n + tile]) for n in tiles], axis=1
            )
            red[here, :] = (forward * pivot_ref[...]).astype(jnp.bfloat16)
            up_out[here, :] = dot_nt(forward.astype(jnp.bfloat16), link[...]).astype(jnp.bfloat16)
            for q in range(batch // rows):
                up_copy(b * (batch // rows) + q).start()
            return carry

        lax.fori_loop(0, total // batch, first, 0)

    for n in tiles:
        gain[:, n : n + tile] = dot_nn(link[:, n:], factor[n:, n : n + tile]).astype(jnp.bfloat16)

    @pl.when(middle)
    def _():
        for m in tiles:
            for n in tiles:
                gain_t[n : n + tile, m : m + tile] = gain[m : m + tile, n : n + tile].T

    @pl.when(has_down)
    def _():
        for m in tiles:
            for n in tiles:
                if m >= n:
                    turned = factor[m : m + tile, n : n + tile].T
                    scaled = turned.astype(jnp.float32) * pivot_ref[:, m : m + tile]
                    scaled_t[n : n + tile, m : m + tile] = scaled.astype(jnp.bfloat16)
        for m in tiles:
            for n in tiles:
                k = max(m, n)
                inner[m : m + tile, n : n + tile] = dot_nn(
                    scaled_t[m : m + tile, k:], factor[k:, n : n + tile]
                ).astype(jnp.bfloat16)

    @pl.when(bottom)
    def _():
        def own_part(b, carry):
            here = big(b)
            kept[here, :] = jnp.concatenate([dot_nn(red[here, n:], factor[n:, n : n + tile]) for n in tiles], axis=1)
            return carry

        lax.fori_loop(0, total // batch, own_part, 0)

    own_offset = offsets_ref[s, j]
    below = jnp.minimum(s + 1, levels - 1)
    from_own = (offsets_ref[below, j] == 0).astype(jnp.float32)
    from_side = (offsets_ref[below, jnp.maximum(j - 1, 0)] == 1).astype(jnp.float32)
    parent_own = (own_offset == 0).astype(jnp.float32)
    parent_side = (own_offset == 1).astype(jnp.float32)

    def parent_rows(here):
        return (
            dn_own[here, :].astype(jnp.float32) * parent_own + dn_side[here, :].astype(jnp.float32) * parent_side
        ).astype(jnp.bfloat16)

    def incoming_rows(here):
        return up_own[here, :].astype(jnp.float32) * from_own + up_side[here, :].astype(jnp.float32) * from_side

    @pl.when(top)
    def _():
        @pl.when(has_right)
        def _():
            above_copy().wait_recv()

        def own_part(b, carry):
            here = big(b)
            kept[here, :] = dot_nn(given[here, :].astype(jnp.bfloat16), inner[...]) - dot_nn(
                parent_rows(here), gain[...]
            )
            return carry

        lax.fori_loop(0, total // batch, own_part, 0)

    def forward_top(p):
        here = piece(p)
        result = kept[here, :] - dot_nn(incoming_rows(here).astype(jnp.bfloat16), inner[...])
        dn_out[here, :] = result.astype(jnp.bfloat16)
        dn_copy(p).start()
        out_ref[here, :] = result

    def forward(p):
        here = piece(p)
        reduced = (given[here, :] - incoming_rows(here)).astype(jnp.bfloat16)
        up_out[here, :] = dot_nn(reduced, gain_t[...]).astype(jnp.bfloat16)
        up_copy(p).start()
        red[here, :] = reduced

    def own_part(b):
        here = big(b)
        kept[here, :] = dot_nn(red[here, :], inner[...])

    def backward(p):
        here = piece(p)
        result = kept[here, :] - dot_nn(parent_rows(here), gain[...])

        @pl.when(has_down)
        def _():
            dn_out[here, :] = result.astype(jnp.bfloat16)
            dn_copy(p).start()

        out_ref[here, :] = result

    odd = lax.rem(j, 2)
    up_ahead = jnp.where((odd == 0) & has_left, AHEAD, 0)
    dn_ahead = jnp.where((odd == 1) & has_right, AHEAD, 0)
    lag = jnp.where(bottom, 0, LAG + LAG_STEP * (s - 1))
    group = batch // rows

    def within(p):
        return (p >= 0) & (p < pieces)

    def turn(u, carry):
        @pl.when(has_down & (u < pieces))
        def _():
            up_copy(u).wait_recv()

            @pl.when(has_right)
            def _():
                up_relay(u).start()

        f = u - up_ahead

        @pl.when(has_down & within(f))
        def _():
            @pl.when(has_left)
            def _():
                up_relay(f).wait_recv()

            @pl.when(top)
            def _():
                forward_top(f)

            @pl.when(middle)
            def _():
                forward(f)

        r = u - lag

        @pl.when(has_up & within(r))
        def _():
            dn_copy(r).wait_recv()

            @pl.when(has_left)
            def _():
                dn_relay(r).start()

        b = r - dn_ahead

        @pl.when(has_up & within(b))
        def _():
            @pl.when(has_right)
            def _():
                dn_relay(b).wait_recv()

            backward(b)

        @pl.when(middle & within(f) & (lax.rem(f, group) == group - 1))
        def _():
            own_part(lax.div(f, group))

        return carry

    turns = jnp.where(top, pieces + up_ahead, pieces + lag + dn_ahead)
    lax.fori_loop(0, turns, turn, 0)

    def finish(p, carry):
        @pl.when(has_up)
        def _():
            up_copy(p).wait_send()

            @pl.when(has_left)
            def _():
                dn_relay(p).wait_send()

        @pl.when(has_down)
        def _():
            dn_copy(p).wait_send()

            @pl.when(has_right)
            def _():
                up_relay(p).wait_send()

        return carry

    lax.fori_loop(0, pieces, finish, 0)

    @pl.when(top & has_left)
    def _():
        above_copy().wait_send()


def local(
    right_side,
    inverse_raw,
    inverse_pattern,
    coupling,
    coupling_pattern,
    pivots,
    offsets,
    above_solution,
):
    levels = lax.axis_size("section")
    nodes = lax.axis_size("scen")
    total, features = right_side.shape[2:]
    rows = min(ROWS, total)
    pieces = total // rows
    vmem = pl.BlockSpec(memory_space=pltpu.VMEM)
    hbm = pl.BlockSpec(memory_space=pl.ANY)
    half = pltpu.VMEM((total, features), jnp.bfloat16)
    whole = pltpu.VMEM((total, features), jnp.float32)
    square = pltpu.VMEM((features, features), jnp.bfloat16)
    sems = pltpu.SemaphoreType.DMA((2, pieces))
    solved = pl.pallas_call(
        functools.partial(kernel, levels, nodes, rows),
        out_shape=pltpu.VMEM((total, features), jnp.float32),
        in_specs=[hbm, hbm, vmem, hbm, vmem, vmem, pl.BlockSpec(memory_space=pltpu.SMEM), hbm],
        out_specs=vmem,
        scratch_shapes=[whole]
        + [square] * 6
        + [whole]
        + [half] * 7
        + [pltpu.SemaphoreType.DMA((4,))]
        + [sems] * 4
        + [pltpu.SemaphoreType.DMA((2,))],
        compiler_params=pltpu.CompilerParams(
            collective_id=0, has_side_effects=True, vmem_limit_bytes=60 * 1024 * 1024
        ),
    )(
        right_side[0, 0],
        inverse_raw[0, 0],
        inverse_pattern[0, 0],
        coupling[0, 0],
        coupling_pattern[0, 0],
        pivots[0],
        offsets,
        above_solution[0],
    )
    return solved[None, None]


def solution(mesh):
    placed = (
        P("section", "scen", None, None),
        P("section", "scen", None, None),
        P("section", "scen", None, None),
        P("section", "scen", None, None),
        P("section", "scen", None, None),
        P("section", "scen", None),
        P(),
        P("scen", None, None),
    )
    return jax.shard_map(
        local,
        mesh=mesh,
        in_specs=placed,
        out_specs=P("section", "scen", None, None),
        check_vma=False,
    )
```

time: 82 us -> 89.9 us (1.096)
  Pallas kernels: 80.6 us -> 88.4 us
    pallas_call x1, Pallas kernels: 80.6 us -> 88.4 us  [local(): pl.pallas_call(functools.partial(kernel, levels, nodes, rows), out_shape=...]
where the time goes in v1:
time: 89.9 us; the launch traced here: 89.7 us
  Pallas kernels  88.4 us (98%)
  local copies, waits for them, and re-layouts  1.32 us (1%)
    pallas_call x1, Pallas kernels, local(): pl.pallas_call(functools.partial(kernel, levels, nodes, rows), out_shape=...  88.4 us

profile of v1, /device:TPU:7, one launch (start us, length us, event | category | flops | bytes accessed | tf_op | source)
XLA Modules:
  0.0 89.7 jit_solution(8871661871932308419)
XLA Ops:
  0.0 88.4 %shard_map.82 = f32[512,1024]{1,0:T(8,128)S(1)} custom-call(f32[512,1024]{1,0:T(8,128)} %bitcast.9, bf16[1024,1024]{1,0:T(8,128)(2,1)} %bitcast.10, s32[16,16]{1,0:T(8,128)} %bitcast.13, bf16[1024,1024]{1,0:T(8,128)(2,1)} %bitcast.11, s32[16,16]{1,0:T(8,128)} %bitcast.14, f32[1,1024]{1,0:T(1,128)} %bitcast.15, s32[4,8]{1,0:T(4,128)} %offsets_ref.1, ...), custom_call_target="tpu_custom_call" | custom-call | tf_op jit(solution)/shard_map/pallas_call | solution.py:406
  88.4 1.3 %copy.10 = f32[1,1,512,1024]{3,2,1,0:T(8,128)} copy(f32[1,1,512,1024]{3,2,1,0:T(8,128)S(1)} %bitcast.8) | data formatting | bytes 4194304

commit v2 on v1

--- a/solution.py
+++ b/solution.py
@@ -8,12 +8,12 @@
 from jax.sharding import PartitionSpec as P
 
 ROWS = 32
+SMALL = 16
+COUNT = 0
 BATCH = 128
 TILE = 256
 LANE = 128
-AHEAD = 2
-LAG = 7
-LAG_STEP = 7
+ROUTES = ((1, 2, 0, 256),)
 MESH = pl.DeviceIdType.MESH
 
 
@@ -23,12 +23,82 @@
 
 def dot_nt(a, b):
     return lax.dot_general(a, b, (((1,), (1,)), ((), ())), preferred_element_type=jnp.float32)
+
+
+RELAY_UP, RELAY_DOWN, FORWARD, BACKWARD, OWN, PASS_UP, PASS_DOWN = range(7)
+KINDS = 8
+DIGITS = 10
+
+
+def piece_rows(total):
+    count = COUNT if total >= COUNT * SMALL + ROWS else 0
+    sizes = [SMALL] * count + [min(ROWS, total)] * ((total - count * SMALL) // min(ROWS, total))
+    starts = [sum(sizes[:p]) for p in range(len(sizes))]
+    return count, sizes, starts
+
+
+def routed_piece(a, b, start):
+    return any((a, b) == (src, dst) and low <= start < high for src, dst, low, high in ROUTES)
+
+
+def orders(levels, sizes, starts, batch):
+    pieces = len(sizes)
+    wire = [0.022 * size for size in sizes]
+    far, near, work = 2.25, 1.1, 0.6
+    steps = {(s, o): [] for s in range(levels) for o in (0, 1)}
+    group = [start // batch for start in starts]
+
+    def hop(a, b, time, o, p):
+        time += far + 2 * wire[p]
+        if routed_piece(a, b, starts[p]):
+            steps[(a + levels // 2) % levels, o].append((time, 0, PASS_UP if b < a else PASS_DOWN, p))
+            time += far + 2 * wire[p]
+        return time + (0.5 if {a, b} == {1, 2} else 0.0)
+
+    def stage(s, src, kind, relay, sent):
+        own = [[hop(src, s, sent[o][p], o, p) for p in range(pieces)] for o in (0, 1)]
+        done = [[], []]
+        for o in (0, 1):
+            close = (o == 1) == (relay == RELAY_UP)
+            before = arrived = 0.0
+            for p in range(pieces):
+                arrived = max(arrived, own[o][p])
+                steps[s, o].append((arrived, 1, relay, p))
+                time = max(arrived, own[1 - o][p] + (near if close else far + wire[p]), before)
+                steps[s, o].append((time, 2, kind, p))
+                before = time + work
+                done[o].append(before)
+        return done
+
+    sent = [[4.0 + 0.0444 * start for start in starts]] * 2
+    for s in range(levels - 2, -1, -1):
+        sent = stage(s, s + 1, FORWARD, RELAY_UP, sent)
+        if s > 0:
+            for o in (0, 1):
+                for g in range(group[-1] + 1):
+                    end = max(sent[o][p] for p in range(pieces) if group[p] == g)
+                    steps[s, o].append((end + 0.5, 3, OWN, g))
+    for s in range(1, levels):
+        sent = stage(s, s - 1, BACKWARD, RELAY_DOWN, sent)
+    ordered = {}
+    for key, listed in steps.items():
+        rows_done, taken = set(), []
+        for _, _, kind, p in sorted(listed):
+            if kind == BACKWARD and key[0] < levels - 1 and group[p] not in rows_done:
+                rows_done.add(group[p])
+                taken.append(OWN)
+            if kind == OWN:
+                if p in rows_done:
+                    continue
+                rows_done.add(p)
+            taken.append(kind)
+        ordered[key] = taken
+    return ordered
 
 
 def kernel(
     levels,
     nodes,
-    rows,
     given_hbm,
     raw_hbm,
     pattern_ref,
@@ -53,17 +123,22 @@
     dn_out,
     dn_own,
     dn_side,
+    up_pass,
+    dn_pass,
     load_sems,
     up_sems,
     up_side_sems,
     dn_sems,
     dn_side_sems,
+    up_pass_sems,
+    dn_pass_sems,
     above_sems,
 ):
     s = lax.axis_index("section")
     j = lax.axis_index("scen")
     total, features = given.shape
-    pieces = total // rows
+    count, sizes, starts = piece_rows(total)
+    pieces = len(sizes)
     batch = min(BATCH, total)
     blocks = pattern_ref.shape[0]
     size = features // blocks
@@ -92,39 +167,122 @@
         load_above.start()
 
     barrier = pltpu.get_barrier_semaphore()
-    count = jnp.int32(0)
-    for has, where_to in ((has_up, up_id), (has_down, down_id), (has_left, left_id), (has_right, right_id)):
+    for step in range(1, levels):
+        pl.semaphore_signal(
+            barrier, inc=1, device_id={"section": lax.rem(s + step, levels)}, device_id_type=MESH
+        )
+    for has, where_to in ((has_left, left_id), (has_right, right_id)):
 
         @pl.when(has)
         def _(where_to=where_to):
             pl.semaphore_signal(barrier, inc=1, device_id=where_to, device_id_type=MESH)
 
-        count = count + has.astype(jnp.int32)
-
-    def piece(p):
-        return pl.ds(pl.multiple_of(p * rows, rows), rows)
-
-    def copy(src, dst, sems, p, device):
+    greeted = levels - 1 + has_left.astype(jnp.int32) + has_right.astype(jnp.int32)
+
+    def sized(p, act):
+        if isinstance(p, int):
+            act(p, pl.ds(starts[p], sizes[p]))
+            return
+        rows = sizes[-1]
+        if count:
+
+            @pl.when(p < count)
+            def _():
+                act(p, pl.ds(pl.multiple_of(p * SMALL, SMALL), SMALL))
+
+            @pl.when(p >= count)
+            def _():
+                act(p, pl.ds(pl.multiple_of(count * SMALL + (p - count) * rows, SMALL), rows))
+
+        else:
+            act(p, pl.ds(pl.multiple_of(p * rows, rows), rows))
+
+    def copy(src, dst, send_sem, recv_sem, here, device):
         return pltpu.make_async_remote_copy(
-            src_ref=src.at[piece(p), :],
-            dst_ref=dst.at[piece(p), :],
-            send_sem=sems.at[0, p],
-            recv_sem=sems.at[1, p],
+            src_ref=src.at[here, :],
+            dst_ref=dst.at[here, :],
+            send_sem=send_sem,
+            recv_sem=recv_sem,
             device_id=device,
             device_id_type=MESH,
         )
 
-    def up_copy(p):
-        return copy(up_out, up_own, up_sems, p, up_id)
-
-    def up_relay(p):
-        return copy(up_own, up_side, up_side_sems, p, right_id)
-
-    def dn_copy(p):
-        return copy(dn_out, dn_own, dn_sems, p, down_id)
-
-    def dn_relay(p):
-        return copy(dn_own, dn_side, dn_side_sems, p, left_id)
+    def up_copy(p, here):
+        return copy(up_out, up_own, up_sems.at[0, p], up_sems.at[1, p], here, up_id)
+
+    def up_relay(p, here):
+        return copy(up_own, up_side, up_side_sems.at[0, p], up_side_sems.at[1, p], here, right_id)
+
+    def dn_copy(p, here):
+        return copy(dn_out, dn_own, dn_sems.at[0, p], dn_sems.at[1, p], here, down_id)
+
+    def dn_relay(p, here):
+        return copy(dn_own, dn_side, dn_side_sems.at[0, p], dn_side_sems.at[1, p], here, left_id)
+
+    middle_id = {"section": lax.rem(s + levels // 2, levels)}
+    origin = lax.rem(s + levels // 2, levels)
+
+    def up_detour(p, here):
+        return copy(up_out, up_pass, up_sems.at[0, p], up_pass_sems.at[1, p], here, middle_id)
+
+    def up_on(p, here):
+        device = {"section": lax.rem(origin + levels - 1, levels)}
+        return copy(up_pass, up_own, up_pass_sems.at[0, p], up_sems.at[1, p], here, device)
+
+    def dn_detour(p, here):
+        return copy(dn_out, dn_pass, dn_sems.at[0, p], dn_pass_sems.at[1, p], here, middle_id)
+
+    def dn_on(p, here):
+        device = {"section": lax.rem(origin + 1, levels)}
+        return copy(dn_pass, dn_own, dn_pass_sems.at[0, p], dn_sems.at[1, p], here, device)
+
+    def row_of(p):
+        return p * SMALL if count == 0 and sizes[-1] == SMALL else jnp.where(
+            p < count, p * SMALL, count * SMALL + (p - count) * sizes[-1]
+        )
+
+    def routed(a, upward, p):
+        found = jnp.bool_(False)
+        start = row_of(p)
+        for src, dst, low, high in ROUTES:
+            if (dst < src) == upward:
+                found = found | ((a == src) & (start >= low) & (start < high))
+        return found
+
+    def send(p, here, upward):
+        straight, detour = (up_copy, up_detour) if upward else (dn_copy, dn_detour)
+        if not any((dst < src) == upward for src, dst, _, _ in ROUTES):
+            straight(p, here).start()
+            return
+        round_about = routed(s, upward, p)
+
+        @pl.when(round_about)
+        def _():
+            detour(p, here).start()
+
+        @pl.when(jnp.logical_not(round_about))
+        def _():
+            straight(p, here).start()
+
+    odd = lax.rem(j, 2)
+    listed = orders(levels, sizes, starts, batch)
+    turns = jnp.int32(0)
+    words = [jnp.int32(0)] * -(-max(len(steps) for steps in listed.values()) // DIGITS)
+    for (section, parity), steps in listed.items():
+        mine = (s == section) & (odd == parity)
+        turns = jnp.where(mine, len(steps), turns)
+        for w in range(len(words)):
+            digits = steps[w * DIGITS : (w + 1) * DIGITS]
+            packed = sum(kind * KINDS**i for i, kind in enumerate(digits))
+            words[w] = jnp.where(mine, packed, words[w])
+
+    def first_routed(upward):
+        found = jnp.int32(0)
+        for src, dst, low, high in ROUTES:
+            if (dst < src) == upward:
+                p = sum(start < low for start in starts)
+                found = jnp.where(lax.rem(src + levels // 2, levels) == s, p, found)
+        return found
 
     def above_copy():
         return pltpu.make_async_remote_copy(
@@ -172,7 +330,7 @@
         mask = jnp.broadcast_to(link_mask[i : i + 1, :], (size, features)).astype(jnp.bfloat16)
         link[part, :] = link[part, :] * mask
     loads[1].wait()
-    pl.semaphore_wait(barrier, count)
+    pl.semaphore_wait(barrier, greeted)
 
     @pl.when(top)
     def _():
@@ -185,21 +343,36 @@
     def big(b):
         return pl.ds(pl.multiple_of(b * batch, batch), batch)
 
+    def first_terms(here):
+        given_rows = given[here, :].astype(jnp.bfloat16)
+        forward = jnp.concatenate(
+            [dot_nt(given_rows[:, : n + tile], factor[n : n + tile, : n + tile]) for n in tiles], axis=1
+        )
+        red[here, :] = (forward * pivot_ref[...]).astype(jnp.bfloat16)
+        up_out[here, :] = dot_nt(forward.astype(jnp.bfloat16), link[...]).astype(jnp.bfloat16)
+
     @pl.when(bottom)
     def _():
+        begin = 0
+        for end in (sizes[-1], batch):
+            if end > begin:
+                first_terms(pl.ds(begin, end - begin))
+                for p in range(pieces):
+                    if begin <= starts[p] < end:
+                        sized(p, lambda p, here: send(p, here, True))
+            begin = end
+        head = sum(start < batch for start in starts)
+        per_batch = batch // sizes[-1]
+
         def first(b, carry):
-            here = big(b)
-            given_rows = given[here, :].astype(jnp.bfloat16)
-            forward = jnp.concatenate(
-                [dot_nt(given_rows[:, : n + tile], factor[n : n + tile, : n + tile]) for n in tiles], axis=1
-            )
-            red[here, :] = (forward * pivot_ref[...]).astype(jnp.bfloat16)
-            up_out[here, :] = dot_nt(forward.astype(jnp.bfloat16), link[...]).astype(jnp.bfloat16)
-            for q in range(batch // rows):
-                up_copy(b * (batch // rows) + q).start()
+            first_terms(big(b))
+            for q in range(per_batch):
+                p = head + (b - 1) * per_batch + q
+                here = pl.ds(pl.multiple_of(b * batch + q * sizes[-1], sizes[-1]), sizes[-1])
+                send(p, here, True)
             return carry
 
-        lax.fori_loop(0, total // batch, first, 0)
+        lax.fori_loop(1, total // batch, first, 0)
 
     for n in tiles:
         gain[:, n : n + tile] = dot_nn(link[:, n:], factor[n:, n : n + tile]).astype(jnp.bfloat16)
@@ -264,115 +437,136 @@
 
         lax.fori_loop(0, total // batch, own_part, 0)
 
-    def forward_top(p):
-        here = piece(p)
+    def forward_top(p, here):
         result = kept[here, :] - dot_nn(incoming_rows(here).astype(jnp.bfloat16), inner[...])
         dn_out[here, :] = result.astype(jnp.bfloat16)
-        dn_copy(p).start()
+        send(p, here, False)
         out_ref[here, :] = result
 
-    def forward(p):
-        here = piece(p)
+    def forward(p, here):
         reduced = (given[here, :] - incoming_rows(here)).astype(jnp.bfloat16)
         up_out[here, :] = dot_nn(reduced, gain_t[...]).astype(jnp.bfloat16)
-        up_copy(p).start()
+        send(p, here, True)
         red[here, :] = reduced
 
-    def own_part(b):
-        here = big(b)
-        kept[here, :] = dot_nn(red[here, :], inner[...])
-
-    def backward(p):
-        here = piece(p)
+    def backward(p, here):
         result = kept[here, :] - dot_nn(parent_rows(here), gain[...])
 
         @pl.when(has_down)
         def _():
             dn_out[here, :] = result.astype(jnp.bfloat16)
-            dn_copy(p).start()
+            send(p, here, False)
 
         out_ref[here, :] = result
 
-    odd = lax.rem(j, 2)
-    up_ahead = jnp.where((odd == 0) & has_left, AHEAD, 0)
-    dn_ahead = jnp.where((odd == 1) & has_right, AHEAD, 0)
-    lag = jnp.where(bottom, 0, LAG + LAG_STEP * (s - 1))
-    group = batch // rows
-
-    def within(p):
-        return (p >= 0) & (p < pieces)
-
-    def turn(u, carry):
-        @pl.when(has_down & (u < pieces))
-        def _():
-            up_copy(u).wait_recv()
+    def relay_up(p, here):
+        up_copy(p, here).wait_recv()
+
+        @pl.when(has_right)
+        def _():
+            up_relay(p, here).start()
+
+    def relay_down(p, here):
+        dn_copy(p, here).wait_recv()
+
+        @pl.when(has_left)
+        def _():
+            dn_relay(p, here).start()
+
+    def forward_any(p, here):
+        @pl.when(has_left)
+        def _():
+            up_relay(p, here).wait_recv()
+
+        @pl.when(top)
+        def _():
+            forward_top(p, here)
+
+        @pl.when(middle)
+        def _():
+            forward(p, here)
+
+    def backward_any(p, here):
+        @pl.when(has_right)
+        def _():
+            dn_relay(p, here).wait_recv()
+
+        backward(p, here)
+
+    def pass_up(p, here):
+        up_detour(p, here).wait_recv()
+        up_on(p, here).start()
+
+    def pass_down(p, here):
+        dn_detour(p, here).wait_recv()
+        dn_on(p, here).start()
+
+    acts = {RELAY_UP: relay_up, RELAY_DOWN: relay_down, FORWARD: forward_any, BACKWARD: backward_any}
+    if any(dst < src for src, dst, _, _ in ROUTES):
+        acts[PASS_UP] = pass_up
+    if any(dst > src for src, dst, _, _ in ROUTES):
+        acts[PASS_DOWN] = pass_down
+
+    def turn(i, carry):
+        word, counts = carry
+        block = lax.div(i, DIGITS)
+        fresh = words[0]
+        for w in range(1, len(words)):
+            fresh = jnp.where(block == w, words[w], fresh)
+        word = jnp.where(lax.rem(i, DIGITS) == 0, fresh, word)
+        kind = lax.rem(word, KINDS)
+        p = counts[0]
+        for which in range(1, len(counts)):
+            p = jnp.where(kind == which, counts[which], p)
+        for which, act in acts.items():
+
+            @pl.when(kind == which)
+            def _(act=act):
+                sized(p, act)
+
+        @pl.when(kind == OWN)
+        def _():
+            here = big(p)
+            kept[here, :] = dot_nn(red[here, :], inner[...])
+
+        counts = tuple(jnp.where(kind == which, c + 1, c) for which, c in enumerate(counts))
+        return lax.div(word, KINDS), counts
+
+    counts = [jnp.int32(0)] * (KINDS - 1)
+    counts[PASS_UP], counts[PASS_DOWN] = first_routed(True), first_routed(False)
+    lax.fori_loop(0, turns, turn, (jnp.int32(0), tuple(counts)))
+
+    def drain(p, here):
+        @pl.when(has_up)
+        def _():
+            up_copy(p, here).wait_send()
+
+            @pl.when(has_left)
+            def _():
+                dn_relay(p, here).wait_send()
+
+        @pl.when(has_down)
+        def _():
+            dn_copy(p, here).wait_send()
 
             @pl.when(has_right)
             def _():
-                up_relay(u).start()
-
-        f = u - up_ahead
-
-        @pl.when(has_down & within(f))
-        def _():
-            @pl.when(has_left)
+                up_relay(p, here).wait_send()
+
+        if PASS_UP in acts:
+
+            @pl.when(routed(origin, True, p))
             def _():
-                up_relay(f).wait_recv()
-
-            @pl.when(top)
+                up_on(p, here).wait_send()
+
+        if PASS_DOWN in acts:
+
+            @pl.when(routed(origin, False, p))
             def _():
-                forward_top(f)
-
-            @pl.when(middle)
-            def _():
-                forward(f)
-
-        r = u - lag
-
-        @pl.when(has_up & within(r))
-        def _():
-            dn_copy(r).wait_recv()
-
-            @pl.when(has_left)
-            def _():
-                dn_relay(r).start()
-
-        b = r - dn_ahead
-
-        @pl.when(has_up & within(b))
-        def _():
-            @pl.when(has_right)
-            def _():
-                dn_relay(b).wait_recv()
-
-            backward(b)
-
-        @pl.when(middle & within(f) & (lax.rem(f, group) == group - 1))
-        def _():
-            own_part(lax.div(f, group))
-
-        return carry
-
-    turns = jnp.where(top, pieces + up_ahead, pieces + lag + dn_ahead)
-    lax.fori_loop(0, turns, turn, 0)
+                dn_on(p, here).wait_send()
 
     def finish(p, carry):
-        @pl.when(has_up)
-        def _():
-            up_copy(p).wait_send()
-
-            @pl.when(has_left)
-            def _():
-                dn_relay(p).wait_send()
-
-        @pl.when(has_down)
-        def _():
-            dn_copy(p).wait_send()
-
-            @pl.when(has_right)
-            def _():
-                up_relay(p).wait_send()
-
+        sized(p, drain)
         return carry
 
     lax.fori_loop(0, pieces, finish, 0)
@@ -395,8 +589,8 @@
     levels = lax.axis_size("section")
     nodes = lax.axis_size("scen")
     total, features = right_side.shape[2:]
-    rows = min(ROWS, total)
-    pieces = total // rows
+    _, sizes, starts = piece_rows(total)
+    pieces = len(sizes)
     vmem = pl.BlockSpec(memory_space=pltpu.VMEM)
     hbm = pl.BlockSpec(memory_space=pl.ANY)
     half = pltpu.VMEM((total, features), jnp.bfloat16)
@@ -404,16 +598,16 @@
     square = pltpu.VMEM((features, features), jnp.bfloat16)
     sems = pltpu.SemaphoreType.DMA((2, pieces))
     solved = pl.pallas_call(
-        functools.partial(kernel, levels, nodes, rows),
+        functools.partial(kernel, levels, nodes),
         out_shape=pltpu.VMEM((total, features), jnp.float32),
         in_specs=[hbm, hbm, vmem, hbm, vmem, vmem, pl.BlockSpec(memory_space=pltpu.SMEM), hbm],
         out_specs=vmem,
         scratch_shapes=[whole]
         + [square] * 6
         + [whole]
-        + [half] * 7
+        + [half] * 9
         + [pltpu.SemaphoreType.DMA((4,))]
-        + [sems] * 4
+        + [sems] * 6
         + [pltpu.SemaphoreType.DMA((2,))],
         compiler_params=pltpu.CompilerParams(
             collective_id=0, has_side_effects=True, vmem_limit_bytes=60 * 1024 * 1024

time: 89.9 us -> 73.7 us (0.82)
  Pallas kernels: 88.4 us -> 72.2 us
    pallas_call x1, Pallas kernels: 88.4 us -> 72.2 us  [local(): pl.pallas_call(functools.partial(kernel, levels, nodes), out_shape=pltpu....]
where the time goes in v2:
time: 73.7 us; the launch traced here: 73.5 us
  Pallas kernels  72.2 us (98%)
  local copies, waits for them, and re-layouts  1.32 us (2%)
    pallas_call x1, Pallas kernels, local(): pl.pallas_call(functools.partial(kernel, levels, nodes), out_shape=pltpu....  72.2 us

profile of v2, /device:TPU:7, one launch (start us, length us, event | category | flops | bytes accessed | tf_op | source)
XLA Modules:
  0.0 73.5 jit_solution(7470666168263852888)
XLA Ops:
  0.0 72.2 %shard_map.82 = f32[512,1024]{1,0:T(8,128)S(1)} custom-call(f32[512,1024]{1,0:T(8,128)} %bitcast.9, bf16[1024,1024]{1,0:T(8,128)(2,1)} %bitcast.10, s32[16,16]{1,0:T(8,128)} %bitcast.13, bf16[1024,1024]{1,0:T(8,128)(2,1)} %bitcast.11, s32[16,16]{1,0:T(8,128)} %bitcast.14, f32[1,1024]{1,0:T(1,128)} %bitcast.15, s32[4,8]{1,0:T(4,128)} %offsets_ref.1, ...), custom_call_target="tpu_custom_call" | custom-call | tf_op jit(solution)/shard_map/pallas_call | solution.py:600
  72.2 1.3 %copy.10 = f32[1,1,512,1024]{3,2,1,0:T(8,128)} copy(f32[1,1,512,1024]{3,2,1,0:T(8,128)S(1)} %bitcast.8) | data formatting | bytes 4194304

commit v3 on v1

v3 whole, which is shorter than its diff:
```python
import functools

import jax
import jax.numpy as jnp
from jax import lax
from jax.experimental import pallas as pl
from jax.experimental.pallas import tpu as pltpu
from jax.sharding import PartitionSpec as P

ROWS = 32
CHUNKS = 1
BATCH = 128
TILE = 256
LANE = 128
ROUTES = ((1, 2, 0, 256), (2, 3, 288, 320))
MESH = pl.DeviceIdType.MESH


def dot_nn(a, b):
    return lax.dot_general(a, b, (((1,), (0,)), ((), ())), preferred_element_type=jnp.float32)


def dot_nt(a, b):
    return lax.dot_general(a, b, (((1,), (1,)), ((), ())), preferred_element_type=jnp.float32)


RELAY_UP, RELAY_DOWN, FORWARD, BACKWARD, OWN, PASS_UP, PASS_DOWN = range(7)
KINDS = 8
DIGITS = 10


ACROSS, CORNER, FAR, NEAR, WORK, EVERY, FIRST, DETOUR, LATER, CHUNK = (4.03, 0.39, 3.47, 1.27, 0.89, 1.68, 3.24, 2.84, 0.23, 0.0)


def routed_piece(a, b, start):
    return any((a, b) == (src, dst) and low <= start < high for src, dst, low, high in ROUTES)


def orders(levels, pieces, rows, batch):
    steps = {(s, o): [] for s in range(levels) for o in (0, 1)}
    chunks = range(CHUNKS)
    group = batch // rows

    def hop(a, b, time, o, p, q):
        if routed_piece(a, b, p * rows):
            kind = PASS_UP if b < a else PASS_DOWN
            steps[(a + levels // 2) % levels, o].append((time + ACROSS, 0, kind, p * CHUNKS + q))
            time += DETOUR
        return time + ACROSS + (CORNER if {a, b} == {1, 2} else 0.0)

    def stage(s, src, kind, relay, sent):
        own = [[[hop(src, s, sent[o][p][q], o, p, q) for q in chunks] for p in range(pieces)] for o in (0, 1)]
        done = [[], []]
        for o in (0, 1):
            side = NEAR if (o == 1) == (relay == RELAY_UP) else FAR
            before = arrived = 0.0
            for p in range(pieces):
                for q in chunks:
                    arrived = max(arrived, own[o][p][q])
                    steps[s, o].append((arrived, 1, relay, p * CHUNKS + q))
                early = max(own[o][p][0], own[1 - o][p][0] + side, before)
                time = max(arrived, own[1 - o][p][-1] + side, before)
                if CHUNKS > 1:
                    time = max(time - WORK / CHUNKS, early)
                steps[s, o].append((time, 2, kind, p))
                before = time + WORK
                done[o].append([time + WORK * (0.75 + 0.25 * q if CHUNKS > 1 else 1.0) for q in chunks])
        return done

    sent = [[[FIRST + EVERY * p + CHUNK * q for q in chunks] for p in range(pieces)]] * 2
    for s in range(levels - 2, -1, -1):
        sent = stage(s, s + 1, FORWARD, RELAY_UP, sent)
        if s > 0:
            for o in (0, 1):
                for g in range(pieces // group):
                    steps[s, o].append((sent[o][(g + 1) * group - 1][-1] + LATER, 3, OWN, g))
    for s in range(1, levels):
        sent = stage(s, s - 1, BACKWARD, RELAY_DOWN, sent)
    ordered = {}
    for key, listed in steps.items():
        parts_done, taken = set(), []
        for _, _, kind, p in sorted(listed):
            if kind == BACKWARD and key[0] < levels - 1 and p // group not in parts_done:
                parts_done.add(p // group)
                taken.append(OWN)
            if kind == OWN:
                if p in parts_done:
                    continue
                parts_done.add(p)
            taken.append(kind)
        ordered[key] = taken
    return ordered


def kernel(
    levels,
    nodes,
    given_hbm,
    raw_hbm,
    pattern_hbm,
    coupling_hbm,
    coupling_pattern_hbm,
    pivot_hbm,
    offsets_hbm,
    above_hbm,
    out_ref,
    given,
    factor,
    link,
    gain,
    gain_t,
    inner,
    scaled_t,
    kept,
    red,
    up_out,
    up_own,
    up_side,
    dn_out,
    dn_own,
    dn_side,
    up_pass,
    dn_pass,
    pattern_ref,
    coupling_pattern_ref,
    pivot_ref,
    offsets_ref,
    load_sems,
    up_sems,
    up_side_sems,
    dn_sems,
    dn_side_sems,
    up_pass_sems,
    dn_pass_sems,
    above_sems,
):
    s = lax.axis_index("section")
    j = lax.axis_index("scen")
    total, features = given.shape
    rows = min(ROWS, total)
    pieces = total // rows
    batch = min(BATCH, total)
    chunk = features // CHUNKS
    spans = [slice(q * chunk, (q + 1) * chunk) for q in range(CHUNKS)]
    blocks = pattern_ref.shape[0]
    size = features // blocks
    tile = min(TILE, features)
    tiles = range(0, features, tile)
    top, bottom = s == 0, s == levels - 1
    middle = jnp.logical_not(top | bottom)
    has_up, has_down = s > 0, s < levels - 1
    has_left, has_right = j > 0, j < nodes - 1
    up_id = {"section": lax.rem(s + levels - 1, levels)}
    down_id = {"section": lax.rem(s + 1, levels)}
    right_id = {"scen": lax.rem(j + 1, nodes)}
    left_id = {"scen": lax.rem(j + nodes - 1, nodes)}

    loads = [
        pltpu.make_async_copy(raw_hbm, factor, load_sems.at[0]),
        pltpu.make_async_copy(given_hbm, given, load_sems.at[1]),
        pltpu.make_async_copy(coupling_hbm, link, load_sems.at[2]),
    ]
    small_loads = [
        pltpu.make_async_copy(src, dst, load_sems.at[4 + i])
        for i, (src, dst) in enumerate(
            (
                (pattern_hbm, pattern_ref),
                (coupling_pattern_hbm, coupling_pattern_ref),
                (pivot_hbm, pivot_ref),
                (offsets_hbm, offsets_ref),
            )
        )
    ]
    above_loads = [
        pltpu.make_async_copy(above_hbm.at[:, span], dn_own.at[q], above_sems.at[2 + q])
        for q, span in enumerate(spans)
    ]

    barrier = pltpu.get_barrier_semaphore()
    for step in range(1, levels):
        pl.semaphore_signal(
            barrier, inc=1, device_id={"section": lax.rem(s + step, levels)}, device_id_type=MESH
        )
    for has, where_to in ((has_left, left_id), (has_right, right_id)):

        @pl.when(has)
        def _(where_to=where_to):
            pl.semaphore_signal(barrier, inc=1, device_id=where_to, device_id_type=MESH)

    for load in small_loads + loads:
        load.start()

    @pl.when(top)
    def _():
        for load in above_loads:
            load.start()

    greeted = levels - 1 + has_left.astype(jnp.int32) + has_right.astype(jnp.int32)

    def piece(p):
        return pl.ds(pl.multiple_of(p * rows, rows), rows)

    def copy(src, dst, send_sems, recv_sems, m, device):
        p, q = lax.div(m, CHUNKS), lax.rem(m, CHUNKS)
        return pltpu.make_async_remote_copy(
            src_ref=src.at[q, piece(p), :],
            dst_ref=dst.at[q, piece(p), :],
            send_sem=send_sems.at[0, m],
            recv_sem=recv_sems.at[1, m],
            device_id=device,
            device_id_type=MESH,
        )

    def up_copy(m):
        return copy(up_out, up_own, up_sems, up_sems, m, up_id)

    def up_relay(m):
        return copy(up_own, up_side, up_side_sems, up_side_sems, m, right_id)

    def dn_copy(m):
        return copy(dn_out, dn_own, dn_sems, dn_sems, m, down_id)

    def dn_relay(m):
        return copy(dn_own, dn_side, dn_side_sems, dn_side_sems, m, left_id)

    def above_copy():
        return pltpu.make_async_remote_copy(
            src_ref=dn_own,
            dst_ref=dn_side,
            send_sem=above_sems.at[0],
            recv_sem=above_sems.at[1],
            device_id=left_id,
            device_id_type=MESH,
        )

    middle_id = {"section": lax.rem(s + levels // 2, levels)}
    origin = lax.rem(s + levels // 2, levels)

    def up_detour(m):
        return copy(up_out, up_pass, up_sems, up_pass_sems, m, middle_id)

    def up_on(m):
        device = {"section": lax.rem(origin + levels - 1, levels)}
        return copy(up_pass, up_own, up_pass_sems, up_sems, m, device)

    def dn_detour(m):
        return copy(dn_out, dn_pass, dn_sems, dn_pass_sems, m, middle_id)

    def dn_on(m):
        device = {"section": lax.rem(origin + 1, levels)}
        return copy(dn_pass, dn_own, dn_pass_sems, dn_sems, m, device)

    def routed(a, upward, p):
        found = jnp.bool_(False)
        for src, dst, low, high in ROUTES:
            if (dst < src) == upward:
                found = found | ((a == src) & (p >= low // rows) & (p < high // rows))
        return found

    def send(p, q, upward):
        m = p * CHUNKS + q
        straight, detour = (up_copy, up_detour) if upward else (dn_copy, dn_detour)
        if not any((dst < src) == upward for src, dst, _, _ in ROUTES):
            straight(m).start()
            return
        round_about = routed(s, upward, p)

        @pl.when(round_about)
        def _():
            detour(m).start()

        @pl.when(jnp.logical_not(round_about))
        def _():
            straight(m).start()

    odd = lax.rem(j, 2)
    listed = orders(levels, pieces, rows, batch)
    turns = jnp.int32(0)
    words = [jnp.int32(0)] * -(-max(len(steps) for steps in listed.values()) // DIGITS)
    for (section, parity), steps in listed.items():
        mine = (s == section) & (odd == parity)
        turns = jnp.where(mine, len(steps), turns)
        for w in range(len(words)):
            digits = steps[w * DIGITS : (w + 1) * DIGITS]
            packed = sum(kind * KINDS**i for i, kind in enumerate(digits))
            words[w] = jnp.where(mine, packed, words[w])

    def routed_messages(upward):
        found = {}
        for src, dst, low, high in sorted(ROUTES):
            if (dst < src) == upward:
                found.setdefault(src, []).append((low // rows * CHUNKS, high // rows * CHUNKS))
        return found

    def routed_message(upward, n):
        m = n
        for src, spans_of in routed_messages(upward).items():
            skipped, total_of, last = 0, 0, 0
            for low, high in spans_of:
                skipped += low - last
                m = jnp.where((origin == src) & (n >= total_of), n + skipped, m)
                total_of += high - low
                last = high
        return m

    @pl.when(jnp.logical_not(has_left))
    def _():
        up_side[...] = jnp.zeros_like(up_side)

    @pl.when(jnp.logical_not(has_right))
    def _():
        dn_side[...] = jnp.zeros_like(dn_side)

    spread = (
        lax.broadcasted_iota(jnp.int32, (blocks, features), 1) // size
        == lax.broadcasted_iota(jnp.int32, (blocks, features), 0)
    ).astype(jnp.bfloat16)
    for load in small_loads:
        load.wait()
    factor_mask = dot_nn(pattern_ref[...].astype(jnp.float32).astype(jnp.bfloat16), spread)
    link_mask = dot_nn(coupling_pattern_ref[...].astype(jnp.float32).astype(jnp.bfloat16), spread)
    loads[0].wait()
    for i in range(blocks):
        part = pl.ds(i * size, size)
        low = i * size // LANE * LANE
        high = (i * size // tile + 1) * tile
        if low > 0:
            mask = jnp.broadcast_to(factor_mask[i : i + 1, :low], (size, low)).astype(jnp.bfloat16)
            factor[part, :low] = factor[part, :low] * mask
        row_ids = lax.broadcasted_iota(jnp.int32, (size, LANE), 0) + i * size
        col_ids = lax.broadcasted_iota(jnp.int32, (size, LANE), 1) + low
        keep = (factor_mask[i : i + 1, low : low + LANE] > 0.5) & (row_ids > col_ids)
        unit = jnp.where(row_ids == col_ids, 1.0, 0.0)
        diagonal = factor[part, low : low + LANE].astype(jnp.float32)
        factor[part, low : low + LANE] = jnp.where(keep, diagonal, unit).astype(jnp.bfloat16)
        if high > low + LANE:
            factor[part, low + LANE : high] = jnp.zeros((size, high - low - LANE), jnp.bfloat16)
    loads[2].wait()
    for i in range(blocks):
        part = pl.ds(i * size, size)
        mask = jnp.broadcast_to(link_mask[i : i + 1, :], (size, features)).astype(jnp.bfloat16)
        link[part, :] = link[part, :] * mask
    loads[1].wait()
    def big(b):
        return pl.ds(pl.multiple_of(b * batch, batch), batch)

    def first_terms(here):
        given_rows = given[here, :].astype(jnp.bfloat16)
        forward = jnp.concatenate(
            [dot_nt(given_rows[:, : n + tile], factor[n : n + tile, : n + tile]) for n in tiles], axis=1
        )
        red[here, :] = (forward * pivot_ref[...]).astype(jnp.bfloat16)
        forward = forward.astype(jnp.bfloat16)
        for q, span in enumerate(spans):
            up_out[q, here, :] = dot_nt(forward, link[span, :]).astype(jnp.bfloat16)

    head_rows = rows if rows < batch else 0

    def send_terms(p):
        for q in range(CHUNKS):
            send(p, q, True)

    @pl.when(bottom)
    def _():
        if head_rows:
            first_terms(pl.ds(0, head_rows))

    pl.semaphore_wait(barrier, greeted)

    @pl.when(top)
    def _():
        for load in above_loads:
            load.wait()

        @pl.when(has_left)
        def _():
            above_copy().start()

    @pl.when(bottom)
    def _():
        for p in range(head_rows // rows):
            send_terms(p)
        first_terms(pl.ds(head_rows, batch - head_rows))
        for p in range(head_rows // rows, batch // rows):
            send_terms(p)

        def first(b, carry):
            first_terms(big(b))
            for p in range(batch // rows):
                send_terms(b * (batch // rows) + p)
            return carry

        lax.fori_loop(1, total // batch, first, 0)

    for n in tiles:
        gain[:, n : n + tile] = dot_nn(link[:, n:], factor[n:, n : n + tile]).astype(jnp.bfloat16)

    @pl.when(middle)
    def _():
        for m in tiles:
            for n in tiles:
                gain_t[n : n + tile, m : m + tile] = gain[m : m + tile, n : n + tile].T

    @pl.when(has_down)
    def _():
        for m in tiles:
            for n in tiles:
                if m >= n:
                    turned = factor[m : m + tile, n : n + tile].T
                    scaled = turned.astype(jnp.float32) * pivot_ref[:, m : m + tile]
                    scaled_t[n : n + tile, m : m + tile] = scaled.astype(jnp.bfloat16)
        for m in tiles:
            for n in tiles:
                k = max(m, n)
                inner[m : m + tile, n : n + tile] = dot_nn(
                    scaled_t[m : m + tile, k:], factor[k:, n : n + tile]
                ).astype(jnp.bfloat16)

    @pl.when(bottom)
    def _():
        def own_part(b, carry):
            here = big(b)
            kept[here, :] = jnp.concatenate([dot_nn(red[here, n:], factor[n:, n : n + tile]) for n in tiles], axis=1)
            return carry

        lax.fori_loop(0, total // batch, own_part, 0)

    own_offset = offsets_ref[s, j]
    below = jnp.minimum(s + 1, levels - 1)
    from_own = (offsets_ref[below, j] == 0).astype(jnp.float32)
    from_side = (offsets_ref[below, jnp.maximum(j - 1, 0)] == 1).astype(jnp.float32)
    parent_own = (own_offset == 0).astype(jnp.float32)
    parent_side = (own_offset == 1).astype(jnp.float32)

    def parent_rows(q, here):
        return (
            dn_own[q, here, :].astype(jnp.float32) * parent_own
            + dn_side[q, here, :].astype(jnp.float32) * parent_side
        ).astype(jnp.bfloat16)

    def incoming_rows(q, here):
        return up_own[q, here, :].astype(jnp.float32) * from_own + up_side[q, here, :].astype(jnp.float32) * from_side

    @pl.when(top)
    def _():
        @pl.when(has_right)
        def _():
            above_copy().wait_recv()

        def own_part(b, carry):
            here = big(b)
            parents = jnp.concatenate([parent_rows(q, here) for q in range(CHUNKS)], axis=1)
            kept[here, :] = dot_nn(given[here, :].astype(jnp.bfloat16), inner[...]) - dot_nn(parents, gain[...])
            return carry

        lax.fori_loop(0, total // batch, own_part, 0)

    def product(chunk_of, matrix, use):
        begun = None
        for q, span in enumerate(spans):
            given_chunk = chunk_of(q)
            if q < CHUNKS - 1:
                partial = dot_nn(given_chunk, matrix[span, :])
                begun = partial if begun is None else begun + partial
            else:
                for n, columns in enumerate(spans):
                    result = dot_nn(given_chunk, matrix[span, columns])
                    use(n, columns, result if begun is None else begun[:, columns] + result)

    def wait_side(relay, exists, p, q):
        @pl.when(exists)
        def _():
            relay(p * CHUNKS + q).wait_recv()

    def forward_top(p):
        here = piece(p)

        def chunk_of(q):
            wait_side(up_relay, has_left, p, q)
            return incoming_rows(q, here).astype(jnp.bfloat16)

        def use(n, columns, value):
            result = kept[here, columns] - value
            dn_out[n, here, :] = result.astype(jnp.bfloat16)
            send(p, n, False)
            out_ref[here, columns] = result

        product(chunk_of, inner, use)

    def forward(p):
        here = piece(p)

        def chunk_of(q):
            wait_side(up_relay, has_left, p, q)
            reduced = (given[here, spans[q]] - incoming_rows(q, here)).astype(jnp.bfloat16)
            red[here, spans[q]] = reduced
            return reduced

        def use(n, columns, value):
            up_out[n, here, :] = value.astype(jnp.bfloat16)
            send(p, n, True)

        product(chunk_of, gain_t, use)

    def backward(p):
        here = piece(p)

        def chunk_of(q):
            wait_side(dn_relay, has_right, p, q)
            return parent_rows(q, here)

        def use(n, columns, value):
            result = kept[here, columns] - value

            @pl.when(has_down)
            def _():
                dn_out[n, here, :] = result.astype(jnp.bfloat16)
                send(p, n, False)

            out_ref[here, columns] = result

        product(chunk_of, gain, use)

    def relay_up(m):
        up_copy(m).wait_recv()

        @pl.when(has_right)
        def _():
            up_relay(m).start()

    def relay_down(m):
        dn_copy(m).wait_recv()

        @pl.when(has_left)
        def _():
            dn_relay(m).start()

    def forward_any(p):
        @pl.when(top)
        def _():
            forward_top(p)

        @pl.when(middle)
        def _():
            forward(p)

    def pass_up(n):
        m = routed_message(True, n)
        up_detour(m).wait_recv()
        up_on(m).start()

    def pass_down(n):
        m = routed_message(False, n)
        dn_detour(m).wait_recv()
        dn_on(m).start()

    def own_part_of(g):
        here = big(g)
        kept[here, :] = dot_nn(red[here, :], inner[...])

    acts = {RELAY_UP: relay_up, RELAY_DOWN: relay_down, FORWARD: forward_any, BACKWARD: backward}
    acts[OWN] = own_part_of
    if any(dst < src for src, dst, _, _ in ROUTES):
        acts[PASS_UP] = pass_up
    if any(dst > src for src, dst, _, _ in ROUTES):
        acts[PASS_DOWN] = pass_down

    def act_on(kinds, kind, counts):
        if len(kinds) == 1:
            acts[kinds[0]](counts[kinds[0]])
            return
        left, right = kinds[: len(kinds) // 2], kinds[len(kinds) // 2 :]

        @pl.when(kind < right[0])
        def _():
            act_on(left, kind, counts)

        @pl.when(kind >= right[0])
        def _():
            act_on(right, kind, counts)

    used = sorted(acts)

    def turn(i, carry):
        word, counts = carry
        kind = lax.rem(word, KINDS)
        act_on(used, kind, dict(zip(used, counts)))
        return lax.div(word, KINDS), tuple(jnp.where(kind == which, c + 1, c) for which, c in zip(used, counts))

    def block(w, counts):
        word = words[0]
        for i in range(1, len(words)):
            word = jnp.where(w == i, words[i], word)
        return lax.fori_loop(0, jnp.minimum(turns - w * DIGITS, DIGITS), turn, (word, counts))[1]

    lax.fori_loop(0, lax.div(turns + DIGITS - 1, DIGITS), block, tuple(jnp.int32(0) for _ in used))

    def finish(m, carry):
        @pl.when(has_up)
        def _():
            up_copy(m).wait_send()

            @pl.when(has_left)
            def _():
                dn_relay(m).wait_send()

        @pl.when(has_down)
        def _():
            dn_copy(m).wait_send()

            @pl.when(has_right)
            def _():
                up_relay(m).wait_send()

        if PASS_UP in acts:

            @pl.when(routed(origin, True, lax.div(m, CHUNKS)))
            def _():
                up_on(m).wait_send()

        if PASS_DOWN in acts:

            @pl.when(routed(origin, False, lax.div(m, CHUNKS)))
            def _():
                dn_on(m).wait_send()

        return carry

    lax.fori_loop(0, pieces * CHUNKS, finish, 0)

    @pl.when(top & has_left)
    def _():
        above_copy().wait_send()


def local(
    right_side,
    inverse_raw,
    inverse_pattern,
    coupling,
    coupling_pattern,
    pivots,
    offsets,
    above_solution,
):
    levels = lax.axis_size("section")
    nodes = lax.axis_size("scen")
    total, features = right_side.shape[2:]
    pieces = total // min(ROWS, total)
    vmem = pl.BlockSpec(memory_space=pltpu.VMEM)
    hbm = pl.BlockSpec(memory_space=pl.ANY)
    half = pltpu.VMEM((total, features), jnp.bfloat16)
    chunked = pltpu.VMEM((CHUNKS, total, features // CHUNKS), jnp.bfloat16)
    whole = pltpu.VMEM((total, features), jnp.float32)
    square = pltpu.VMEM((features, features), jnp.bfloat16)
    sems = pltpu.SemaphoreType.DMA((2, pieces * CHUNKS))
    solved = pl.pallas_call(
        functools.partial(kernel, levels, nodes),
        out_shape=pltpu.VMEM((total, features), jnp.float32),
        in_specs=[hbm] * 8,
        out_specs=vmem,
        scratch_shapes=[whole]
        + [square] * 6
        + [whole]
        + [half]
        + [chunked] * 8
        + [
            pltpu.VMEM(inverse_pattern.shape[2:], jnp.int32),
            pltpu.VMEM(coupling_pattern.shape[2:], jnp.int32),
            pltpu.VMEM((1, features), jnp.float32),
            pltpu.SMEM(offsets.shape, jnp.int32),
        ]
        + [pltpu.SemaphoreType.DMA((8,))]
        + [sems] * 6
        + [pltpu.SemaphoreType.DMA((2 + CHUNKS,))],
        compiler_params=pltpu.CompilerParams(
            collective_id=0, has_side_effects=True, vmem_limit_bytes=60 * 1024 * 1024
        ),
    )(
        right_side[0, 0],
        inverse_raw[0, 0],
        inverse_pattern[0, 0],
        coupling[0, 0],
        coupling_pattern[0, 0],
        pivots[0],
        offsets,
        above_solution[0],
    )
    return solved[None, None]


def solution(mesh):
    placed = (
        P("section", "scen", None, None),
        P("section", "scen", None, None),
        P("section", "scen", None, None),
        P("section", "scen", None, None),
        P("section", "scen", None, None),
        P("section", "scen", None),
        P(),
        P("scen", None, None),
    )
    return jax.shard_map(
        local,
        mesh=mesh,
        in_specs=placed,
        out_specs=P("section", "scen", None, None),
        check_vma=False,
    )
```

time: 89.9 us -> 70.4 us (0.78)
  Pallas kernels: 88.4 us -> 68.7 us
    pallas_call x1, Pallas kernels: 88.4 us -> 68.7 us  [local(): pl.pallas_call(functools.partial(kernel, levels, nodes), out_shape=pltpu....]
where the time goes in v3:
time: 70.4 us; the launch traced here: 70 us
  Pallas kernels  68.7 us (98%)
  local copies, waits for them, and re-layouts  1.32 us (2%)
    pallas_call x1, Pallas kernels, local(): pl.pallas_call(functools.partial(kernel, levels, nodes), out_shape=pltpu....  68.7 us

profile of v3, /device:TPU:7, one launch (start us, length us, event | category | flops | bytes accessed | tf_op | source)
XLA Modules:
  0.0 70.0 jit_solution(15572144769545519632)
XLA Ops:
  0.0 68.7 %shard_map.82 = f32[512,1024]{1,0:T(8,128)S(1)} custom-call(f32[512,1024]{1,0:T(8,128)} %bitcast.9, bf16[1024,1024]{1,0:T(8,128)(2,1)} %bitcast.10, s32[16,16]{1,0:T(8,128)} %bitcast.13, bf16[1024,1024]{1,0:T(8,128)(2,1)} %bitcast.11, s32[16,16]{1,0:T(8,128)} %bitcast.14, f32[1,1024]{1,0:T(1,128)} %bitcast.15, s32[4,8]{1,0:T(4,128)} %offsets_hbm.1, ...), custom_call_target="tpu_custom_call" | custom-call | tf_op jit(solution)/shard_map/pallas_call | solution.py:657
  68.7 1.3 %copy.10 = f32[1,1,512,1024]{3,2,1,0:T(8,128)} copy(f32[1,1,512,1024]{3,2,1,0:T(8,128)S(1)} %bitcast.8) | data formatting | bytes 4194304
